TPU v7x, 512 devices: a whole 4x4x16 slice. The times are simulated.
512 devices in a mesh: ctx: 32 (over z, x_hi), head: 16 (over y, x_lo, core).
Axes of the slice: x: 4 (x_hi: 2, x_lo: 2; x = x_hi * 2 + x_lo), y: 4, z: 16, core: 2. Of those that a mesh axis runs over, the one named last changes fastest.
Arguments:
- query: bfloat16 [65536, 4096], P(('ctx', 'head')), may hold values from -6 to 6
- key: bfloat16 [65536, 2048], P(('ctx', 'head')), may hold values from -6 to 6
- value: bfloat16 [65536, 2048], P(('ctx', 'head')), may hold values from -6 to 6
- out_grad: bfloat16 [65536, 4096], P(('ctx', 'head')), may hold values from -6 to 6
- block_mask: int32 [512, 9], replicated, may hold values from 0 to 1, as said below
Outputs:
- query_grad: bfloat16 [65536, 4096], P(('ctx', 'head'))
- key_grad: bfloat16 [65536, 2048], P(('ctx', 'head'))
- value_grad: bfloat16 [65536, 2048], P(('ctx', 'head'))
Inputs may be any that keep to these rules, and one draw needn't show every extreme that they name: block_mask[b, 0] is 1 for every block b; block_mask[b, o] = 1 lets query block b attend key block b - o.
All inputs are finite; a program needn't handle non-finite values.
Results may differ from a plain program's by a relative error of at most 0.0095.
Values may be sent and summed in bfloat16 or wider, within the bound.
A program may use at most 64 MiB of HBM per device.

v0:
```python
import jax
import jax.numpy as jnp
from jax import lax
from jax.sharding import PartitionSpec as P

HEAD_WIDTH = 128
WINDOW = 1024
BLOCK = 128


PRE_SCALE = 168.0 ** (-0.5)


def shifted(block, axis, distance):
    devices = range(lax.axis_size(axis))
    route = [(i - distance, i) for i in devices if i - distance in devices]
    return lax.ppermute(block, axis, route)


def allowed_mask(mask_rows, n_query, n_key, key_lead, key_first):
    q_index = lax.broadcasted_iota(jnp.int32, (n_query, n_key), 0)
    k_index = lax.broadcasted_iota(jnp.int32, (n_query, n_key), 1)
    gap = key_lead + q_index - k_index
    inside = (gap >= 0) & (gap < WINDOW) & (key_first + k_index >= 0)
    q_blocks = n_query // BLOCK
    k_blocks = n_key // BLOCK
    offsets = mask_rows.shape[1]
    a_index = lax.broadcasted_iota(jnp.int32, (q_blocks, k_blocks, offsets), 0)
    b_index = lax.broadcasted_iota(jnp.int32, (q_blocks, k_blocks, offsets), 1)
    o_index = lax.broadcasted_iota(jnp.int32, (q_blocks, k_blocks, offsets), 2)
    picked = jnp.where(o_index == a_index - b_index + key_lead // BLOCK, mask_rows[:, None, :], 0)
    active = jnp.sum(picked, axis=2) > 0
    active = jnp.repeat(jnp.repeat(active, BLOCK, axis=0), BLOCK, axis=1)
    return inside & active


def scores_of(q_part, k_part, allowed):
    n_query = q_part.shape[0]
    n_key = k_part.shape[0]
    kv_groups = k_part.shape[1] // HEAD_WIDTH
    q_heads = q_part.reshape(n_query, kv_groups, -1, HEAD_WIDTH)
    k_heads = k_part.reshape(n_key, kv_groups, HEAD_WIDTH)
    raw_scores = (
        jnp.einsum("qgrd,kgd->grqk", q_heads, k_heads, preferred_element_type=jnp.float32)
        * PRE_SCALE
    )
    return jnp.where(allowed, raw_scores, -jnp.inf)


def grads_from(probs, q_part, g_part, k_part, v_part, delta):
    n_query = q_part.shape[0]
    n_key = k_part.shape[0]
    kv_groups = k_part.shape[1] // HEAD_WIDTH
    q_heads = q_part.reshape(n_query, kv_groups, -1, HEAD_WIDTH)
    g_heads = g_part.reshape(n_query, kv_groups, -1, HEAD_WIDTH)
    k_heads = k_part.reshape(n_key, kv_groups, HEAD_WIDTH)
    v_heads = v_part.reshape(n_key, kv_groups, HEAD_WIDTH)
    d_value = jnp.einsum(
        "grqk,qgrd->kgd", probs.astype(jnp.bfloat16), g_heads, preferred_element_type=jnp.float32
    )
    d_probs = jnp.einsum("qgrd,kgd->grqk", g_heads, v_heads, preferred_element_type=jnp.float32)
    d_scores = (probs * (d_probs - delta[..., None])).astype(jnp.bfloat16)
    d_key = (
        jnp.einsum("grqk,qgrd->kgd", d_scores, q_heads, preferred_element_type=jnp.float32)
        * PRE_SCALE
    )
    d_query = (
        jnp.einsum("grqk,kgd->qgrd", d_scores, k_heads, preferred_element_type=jnp.float32)
        * PRE_SCALE
    )
    d_query = d_query.reshape(n_query, -1)
    return (d_query, d_key.reshape(n_key, -1), d_value.reshape(n_key, -1))


def tile_pass(q_part, g_part, k_part, v_part, allowed):
    n_query = q_part.shape[0]
    n_key = k_part.shape[0]
    kv_groups = k_part.shape[1] // HEAD_WIDTH
    scores = scores_of(q_part, k_part, allowed)
    row_max = jnp.max(scores, axis=3, keepdims=True)
    row_total = jnp.sum(jnp.exp(scores - row_max), axis=3, keepdims=True)
    log_total = row_max + jnp.log(row_total)
    probs = jnp.exp(scores - log_total)
    v_heads = v_part.reshape(n_key, kv_groups, HEAD_WIDTH)
    attended = jnp.einsum(
        "grqk,kgd->qgrd", probs.astype(jnp.bfloat16), v_heads, preferred_element_type=jnp.float32
    )
    g_heads = g_part.reshape(n_query, kv_groups, -1, HEAD_WIDTH)
    delta = jnp.transpose(jnp.sum(g_heads.astype(jnp.float32) * attended, axis=3), (1, 2, 0))
    d_query, d_key, d_value = grads_from(probs, q_part, g_part, k_part, v_part, delta)
    return (d_query, d_key, d_value, log_total[..., 0], delta)


def on_device(query, key, value, out_grad, block_mask):
    q_seg, k_seg, v_seg, g_seg = (
        lax.all_to_all(query, "head", split_axis=1, concat_axis=0, tiled=True),
        lax.all_to_all(key, "head", split_axis=1, concat_axis=0, tiled=True),
        lax.all_to_all(value, "head", split_axis=1, concat_axis=0, tiled=True),
        lax.all_to_all(out_grad, "head", split_axis=1, concat_axis=0, tiled=True),
    )
    seg_len = q_seg.shape[0]
    tile_rows = BLOCK
    n_tiles = seg_len // tile_rows
    span = tile_rows + WINDOW
    seg_anchor = lax.axis_index("ctx") * seg_len
    own_rows = lax.dynamic_slice_in_dim(block_mask, seg_anchor // BLOCK, seg_len // BLOCK, 0)
    k_prev, v_prev = shifted((k_seg[seg_len - WINDOW :], v_seg[seg_len - WINDOW :]), "ctx", 1)
    k_ext = jnp.concatenate([k_prev, k_seg], 0)
    v_ext = jnp.concatenate([v_prev, v_seg], 0)

    def step_fn(state_pair, tile_index):
        d_key_acc, d_value_acc = state_pair
        first_row = tile_index * tile_rows
        q_part = lax.dynamic_slice_in_dim(q_seg, first_row, tile_rows, 0)
        g_part = lax.dynamic_slice_in_dim(g_seg, first_row, tile_rows, 0)
        k_part = lax.dynamic_slice_in_dim(k_ext, first_row, span, 0)
        v_part = lax.dynamic_slice_in_dim(v_ext, first_row, span, 0)
        mask_rows = lax.dynamic_slice_in_dim(own_rows, first_row // BLOCK, tile_rows // BLOCK, 0)
        allowed = allowed_mask(mask_rows, tile_rows, span, WINDOW, seg_anchor + first_row - WINDOW)
        d_query, d_key, d_value, log_total, delta = tile_pass(
            q_part, g_part, k_part, v_part, allowed
        )
        d_key_acc = lax.dynamic_update_slice_in_dim(
            d_key_acc, lax.dynamic_slice_in_dim(d_key_acc, first_row, span, 0) + d_key, first_row, 0
        )
        d_value_acc = lax.dynamic_update_slice_in_dim(
            d_value_acc,
            lax.dynamic_slice_in_dim(d_value_acc, first_row, span, 0) + d_value,
            first_row,
            0,
        )
        return ((d_key_acc, d_value_acc), (d_query.astype(jnp.bfloat16), log_total, delta))

    tile_ids = jnp.arange(n_tiles, dtype=jnp.int32)
    zero_acc = jnp.zeros((seg_len + WINDOW, k_seg.shape[1]), jnp.float32)
    (d_key_ext, d_value_ext), (d_query, lse_tiles, delta_tiles) = lax.scan(
        step_fn, (zero_acc, zero_acc), tile_ids
    )
    query_grad = d_query.reshape(seg_len, -1)
    key_back, value_back = shifted((d_key_ext[:WINDOW], d_value_ext[:WINDOW]), "ctx", -1)
    lead_zeros = jnp.zeros((seg_len - WINDOW, k_seg.shape[1]), jnp.float32)
    key_grad = (d_key_ext[WINDOW:] + jnp.concatenate([lead_zeros, key_back], 0)).astype(
        jnp.bfloat16
    )
    value_grad = (d_value_ext[WINDOW:] + jnp.concatenate([lead_zeros, value_back], 0)).astype(
        jnp.bfloat16
    )
    return (
        lax.all_to_all(query_grad, "head", split_axis=0, concat_axis=1, tiled=True),
        lax.all_to_all(key_grad, "head", split_axis=0, concat_axis=1, tiled=True),
        lax.all_to_all(value_grad, "head", split_axis=0, concat_axis=1, tiled=True),
    )


def solution(mesh):
    in_specs = (
        P(("ctx", "head"), None),
        P(("ctx", "head"), None),
        P(("ctx", "head"), None),
        P(("ctx", "head"), None),
        P(),
    )
    out_specs = (P(("ctx", "head"), None), P(("ctx", "head"), None), P(("ctx", "head"), None))
    return jax.shard_map(
        on_device, mesh=mesh, in_specs=in_specs, out_specs=out_specs, check_vma=False
    )
```

profile of v0, /device:TPU:1, one launch (start us, length us, event | category | flops | bytes accessed | tf_op | source)
XLA Modules:
  0.0 307.9 jit_solution(4174057927991872316)
XLA Ops:
  2.6 10.2 %all-to-all-start.1 = ((bf16[128,16,128]{2,0,1:T(8,128)(2,1)}), bf16[128,16,128]{2,0,1:T(8,128)(2,1)S(1)}, u32[]{:S(2)}, u32[]{:S(2)}) async-start(bf16[128,16,128]{2,0,1:T(8,128)(2,1)} %copy_bitcast_fusion.1), calls=%async_computation.1 | async-start | bytes 1048576 | tf_op jit(solution)/shard_map/all_to_all | solution.py:97
  13.8 8.8 %all-to-all-done.1 = bf16[128,16,128]{2,0,1:T(8,128)(2,1)S(1)} async-done(((bf16[128,16,128]{2,0,1:T(8,128)(2,1)}), bf16[128,16,128]{2,0,1:T(8,128)(2,1)S(1)}, u32[]{:S(2)}, u32[]{:S(2)}) %all-to-all-start.1) | async-done | bytes 524320 | tf_op jit(solution)/shard_map/all_to_all | solution.py:97
  22.6 4.6 %all-to-all-start.2 = ((bf16[128,16,128]{2,0,1:T(8,128)(2,1)}), bf16[128,16,128]{2,0,1:T(8,128)(2,1)S(1)}, u32[]{:S(2)}, u32[]{:S(2)}) async-start(bf16[128,16,128]{2,0,1:T(8,128)(2,1)} %copy_bitcast_fusion), calls=%async_computation.2 | async-start | bytes 1048576 | tf_op jit(solution)/shard_map/all_to_all | solution.py:98
  27.2 1.3 copy.88
  28.5 8.4 %all-to-all-done.2 = bf16[128,16,128]{2,0,1:T(8,128)(2,1)S(1)} async-done(((bf16[128,16,128]{2,0,1:T(8,128)(2,1)}), bf16[128,16,128]{2,0,1:T(8,128)(2,1)S(1)}, u32[]{:S(2)}, u32[]{:S(2)}) %all-to-all-start.2) | async-done | bytes 524320 | tf_op jit(solution)/shard_map/all_to_all | solution.py:98
  36.9 4.7 %all-to-all-start = ((bf16[128,16,256]{0,2,1:T(8,128)(2,1)}), bf16[128,16,256]{0,2,1:T(8,128)(2,1)S(1)}, u32[]{:S(2)}, u32[]{:S(2)}) async-start(bf16[128,16,256]{0,2,1:T(8,128)(2,1)} %bitcast.32), calls=%async_computation | async-start | bytes 2097152 | tf_op jit(solution)/shard_map/all_to_all | solution.py:96
  41.6 2.3 copy.93
  43.9 13.5 %all-to-all-done = bf16[128,16,256]{0,2,1:T(8,128)(2,1)S(1)} async-done(((bf16[128,16,256]{0,2,1:T(8,128)(2,1)}), bf16[128,16,256]{0,2,1:T(8,128)(2,1)S(1)}, u32[]{:S(2)}, u32[]{:S(2)}) %all-to-all-start) | async-done | bytes 1048608 | tf_op jit(solution)/shard_map/all_to_all | solution.py:96
  57.4 5.0 %all-to-all-start.3 = ((bf16[128,16,256]{0,2,1:T(8,128)(2,1)}), bf16[128,16,256]{0,2,1:T(8,128)(2,1)}, u32[]{:S(2)}, u32[]{:S(2)}) async-start(bf16[128,16,256]{0,2,1:T(8,128)(2,1)} %bitcast.41), calls=%async_computation.3 | async-start | bytes 2097152 | tf_op jit(solution)/shard_map/all_to_all | solution.py:99
  62.5 1.3 collective-permute-start
  64.7 3.5 %collective-permute-start.1 = (bf16[1024,128]{1,0:T(8,128)(2,1)S(1)}, bf16[1024,128]{1,0:T(8,128)(2,1)S(1)}, u32[]{:S(2)}, u32[]{:S(2)}) collective-permute-start(bf16[1024,128]{1,0:T(8,128)(2,1)S(1)} %bitcast.208), channel_id=1, source_target_pairs={{0,16},{16,32},{32,48},{48,64},{64,80},{80,96},{96,112},{112,128},... | collective-permute-start | bytes 786440 | tf_op jit(solution)/shard_map/ppermute | solution.py:17
  68.2 11.6 %collective-permute-done = bf16[1024,128]{1,0:T(8,128)(2,1)S(1)} collective-permute-done((bf16[1024,128]{1,0:T(8,128)(2,1)S(1)}, bf16[1024,128]{1,0:T(8,128)(2,1)S(1)}, u32[]{:S(2)}, u32[]{:S(2)}) %collective-permute-start) | collective-permute-done | bytes 262176 | tf_op jit(solution)/shard_map/ppermute | solution.py:17
  81.5 3.9 %collective-permute-done.1 = bf16[1024,128]{1,0:T(8,128)(2,1)S(1)} collective-permute-done((bf16[1024,128]{1,0:T(8,128)(2,1)S(1)}, bf16[1024,128]{1,0:T(8,128)(2,1)S(1)}, u32[]{:S(2)}, u32[]{:S(2)}) %collective-permute-start.1) | collective-permute-done | bytes 262176 | tf_op jit(solution)/shard_map/ppermute | solution.py:17
  86.3 1.3 copy.89
  87.7 2.3 copy.94
  90.1 1.3 broadcast_in_dim.47
  91.4 140.8 %while.16 = (s32[]{:T(128)}, f32[3072,128]{0,1:T(8,128)}, f32[3072,128]{0,1:T(8,128)S(1)}, bf16[16,128,256]{1,2,0:T(8,128)(2,1)}, s32[16]{0:T(128)S(1)}, /*index...) while((s32[]{:T(128)}, f32[3072,128]{0,1:T(8,128)}, ...), condition=%wide.region_5.6_spmd, body=%wide.region_0.5_spmd.sunk | while | flops 458311840 | bytes 28296552 | solution.py:136
  233.0 1.3 collective-permute-start.3
  234.3 6.1 %all-to-all-start.4 = ((bf16[16,128,256]{1,2,0:T(8,128)(2,1)}), bf16[16,128,256]{1,2,0:T(8,128)(2,1)S(1)}, u32[]{:S(2)}, u32[]{:S(2)}) async-start(bf16[16,128,256]{1,2,0:T(8,128)(2,1)} %get-tuple-element.144), calls=%async_computation.4 | async-start | bytes 2097152 | tf_op jit(solution)/shard_map/all_to_all | solution.py:149
  240.4 1.9 slice.29
  243.6 7.0 %collective-permute-done.3 = f32[1024,128]{0,1:T(8,128)} collective-permute-done((f32[1024,128]{0,1:T(8,128)}, f32[1024,128]{0,1:T(8,128)}, u32[]{:S(2)}, u32[]{:S(2)}) %collective-permute-start.3) | collective-permute-done | bytes 524320 | tf_op jit(solution)/shard_map/ppermute | solution.py:17
  250.6 1.9 add_convert_fusion
  252.5 2.2 copy.100
  254.7 23.3 %all-to-all-done.4 = bf16[16,128,256]{1,2,0:T(8,128)(2,1)S(1)} async-done(((bf16[16,128,256]{1,2,0:T(8,128)(2,1)}), bf16[16,128,256]{1,2,0:T(8,128)(2,1)S(1)}, u32[]{:S(2)}, u32[]{:S(2)}) %all-to-all-start.4) | async-done | bytes 1048608 | tf_op jit(solution)/shard_map/all_to_all | solution.py:149
  278.0 4.4 %all-to-all-start.6 = ((bf16[16,128,128]{2,1,0:T(8,128)(2,1)}), bf16[16,128,128]{2,1,0:T(8,128)(2,1)}, u32[]{:S(2)}, u32[]{:S(2)}) async-start(bf16[16,128,128]{2,1,0:T(8,128)(2,1)} %bitcast.202), calls=%async_computation.6 | async-start | bytes 1048576 | tf_op jit(solution)/shard_map/all_to_all | solution.py:151
  282.4 1.9 add_convert_fusion.1
  284.3 2.0 copy.98
  286.4 5.9 %all-to-all-done.6 = bf16[16,128,128]{2,1,0:T(8,128)(2,1)} async-done(((bf16[16,128,128]{2,1,0:T(8,128)(2,1)}), bf16[16,128,128]{2,1,0:T(8,128)(2,1)}, u32[]{:S(2)}, u32[]{:S(2)}) %all-to-all-start.6) | async-done | bytes 524320 | tf_op jit(solution)/shard_map/all_to_all | solution.py:151
  292.2 4.6 %all-to-all-start.5 = ((bf16[16,128,128]{2,1,0:T(8,128)(2,1)}), bf16[16,128,128]{2,1,0:T(8,128)(2,1)S(1)}, u32[]{:S(2)}, u32[]{:S(2)}) async-start(bf16[16,128,128]{2,1,0:T(8,128)(2,1)} %bitcast.46), calls=%async_computation.5 | async-start | bytes 1048576 | tf_op jit(solution)/shard_map/all_to_all | solution.py:150
  296.9 1.3 copy.114
  298.2 1.3 copy.101
  300.5 6.1 %all-to-all-done.5 = bf16[16,128,128]{2,1,0:T(8,128)(2,1)S(1)} async-done(((bf16[16,128,128]{2,1,0:T(8,128)(2,1)}), bf16[16,128,128]{2,1,0:T(8,128)(2,1)S(1)}, u32[]{:S(2)}, u32[]{:S(2)}) %all-to-all-start.5) | async-done | bytes 524320 | tf_op jit(solution)/shard_map/all_to_all | solution.py:150
  (460 shorter events, 138.8 us)
Async XLA Ops:
  0.6 12.2 %copy-start.6 = (bf16[128,2048]{1,0:T(8,128)(2,1)S(1)}, bf16[128,2048]{1,0:T(8,128)(2,1)}, u32[]{:S(2)}) copy-start(bf16[128,2048]{1,0:T(8,128)(2,1)} %param.9) | copy-start | bytes 1572868
  2.6 20.0 %all-to-all-start.1 = ((bf16[128,16,128]{2,0,1:T(8,128)(2,1)}), bf16[128,16,128]{2,0,1:T(8,128)(2,1)S(1)}, u32[]{:S(2)}, u32[]{:S(2)}) async-start(bf16[128,16,128]{2,0,1:T(8,128)(2,1)} %copy_bitcast_fusion.1), calls=%async_computation.1 | async-start | bytes 1048576 | tf_op jit(solution)/shard_map/all_to_all | solution.py:97
  12.8 14.4 %copy-start.5 = (bf16[128,4096]{1,0:T(8,128)(2,1)S(1)}, bf16[128,4096]{1,0:T(8,128)(2,1)}, u32[]{:S(2)}) copy-start(bf16[128,4096]{1,0:T(8,128)(2,1)} %param.7) | copy-start | bytes 3145732
  22.6 14.4 %all-to-all-start.2 = ((bf16[128,16,128]{2,0,1:T(8,128)(2,1)}), bf16[128,16,128]{2,0,1:T(8,128)(2,1)S(1)}, u32[]{:S(2)}, u32[]{:S(2)}) async-start(bf16[128,16,128]{2,0,1:T(8,128)(2,1)} %copy_bitcast_fusion), calls=%async_computation.2 | async-start | bytes 1048576 | tf_op jit(solution)/shard_map/all_to_all | solution.py:98
  36.9 20.5 %all-to-all-start = ((bf16[128,16,256]{0,2,1:T(8,128)(2,1)}), bf16[128,16,256]{0,2,1:T(8,128)(2,1)S(1)}, u32[]{:S(2)}, u32[]{:S(2)}) async-start(bf16[128,16,256]{0,2,1:T(8,128)(2,1)} %bitcast.32), calls=%async_computation | async-start | bytes 2097152 | tf_op jit(solution)/shard_map/all_to_all | solution.py:96
  57.4 30.3 %all-to-all-start.3 = ((bf16[128,16,256]{0,2,1:T(8,128)(2,1)}), bf16[128,16,256]{0,2,1:T(8,128)(2,1)}, u32[]{:S(2)}, u32[]{:S(2)}) async-start(bf16[128,16,256]{0,2,1:T(8,128)(2,1)} %bitcast.41), calls=%async_computation.3 | async-start | bytes 2097152 | tf_op jit(solution)/shard_map/all_to_all | solution.py:99
  62.5 17.3 %collective-permute-start = (bf16[1024,128]{1,0:T(8,128)(2,1)S(1)}, bf16[1024,128]{1,0:T(8,128)(2,1)S(1)}, u32[]{:S(2)}, u32[]{:S(2)}) collective-permute-start(bf16[1024,128]{1,0:T(8,128)(2,1)S(1)} %bitcast.207), channel_id=1, source_target_pairs={{0,16},{16,32},{32,48},{48,64},{64,80},{80,96},{96,112},{112,128},... | collective-permute-start | bytes 786440 | tf_op jit(solution)/shard_map/ppermute | solution.py:17
  64.7 20.7 %collective-permute-start.1 = (bf16[1024,128]{1,0:T(8,128)(2,1)S(1)}, bf16[1024,128]{1,0:T(8,128)(2,1)S(1)}, u32[]{:S(2)}, u32[]{:S(2)}) collective-permute-start(bf16[1024,128]{1,0:T(8,128)(2,1)S(1)} %bitcast.208), channel_id=1, source_target_pairs={{0,16},{16,32},{32,48},{48,64},{64,80},{80,96},{96,112},{112,128},... | collective-permute-start | bytes 786440 | tf_op jit(solution)/shard_map/ppermute | solution.py:17
  97.3 1.4 copy-start.1
  106.1 1.4 copy-start.1
  114.9 1.4 copy-start.1
  116.6 1.2 copy-start.2
  123.7 1.4 copy-start.1
  132.5 1.4 copy-start.1
  141.3 1.4 copy-start.1
  143.0 1.2 copy-start.2
  150.1 1.4 copy-start.1
  158.9 1.4 copy-start.1
  167.7 1.4 copy-start.1
  176.5 1.4 copy-start.1
  185.3 1.4 copy-start.1
  194.1 1.4 copy-start.1
  202.9 1.4 copy-start.1
  211.7 1.4 copy-start.1
  220.5 1.4 copy-start.1
  229.3 1.4 copy-start.1
  233.0 17.5 %collective-permute-start.3 = (f32[1024,128]{0,1:T(8,128)}, f32[1024,128]{0,1:T(8,128)}, u32[]{:S(2)}, u32[]{:S(2)}) collective-permute-start(f32[1024,128]{0,1:T(8,128)} %slice.31), channel_id=1, source_target_pairs={{16,0},{32,16},{48,32},{64,48},{80,64},{96,80},{112,96},{128,112},... | collective-permute-start | bytes 1572872 | tf_op jit(solution)/shard_map/ppermute | solution.py:17
  234.3 43.6 %all-to-all-start.4 = ((bf16[16,128,256]{1,2,0:T(8,128)(2,1)}), bf16[16,128,256]{1,2,0:T(8,128)(2,1)S(1)}, u32[]{:S(2)}, u32[]{:S(2)}) async-start(bf16[16,128,256]{1,2,0:T(8,128)(2,1)} %get-tuple-element.144), calls=%async_computation.4 | async-start | bytes 2097152 | tf_op jit(solution)/shard_map/all_to_all | solution.py:149
  242.3 40.1 %collective-permute-start.2 = (f32[1024,128]{0,1:T(8,128)}, f32[1024,128]{0,1:T(8,128)}, u32[]{:S(2)}, u32[]{:S(2)}) collective-permute-start(f32[1024,128]{0,1:T(8,128)} %slice.29), channel_id=1, source_target_pairs={{16,0},{32,16},{48,32},{64,48},{80,64},{96,80},{112,96},{128,112},... | collective-permute-start | bytes 1572872 | tf_op jit(solution)/shard_map/ppermute | solution.py:17
  252.5 29.9 %copy-start.3 = (f32[3072,128]{0,1:T(8,128)S(1)}, f32[3072,128]{0,1:T(8,128)}, u32[]{:S(2)}) copy-start(f32[3072,128]{0,1:T(8,128)} %get-tuple-element.145) | copy-start | bytes 4718596
  278.0 14.3 %all-to-all-start.6 = ((bf16[16,128,128]{2,1,0:T(8,128)(2,1)}), bf16[16,128,128]{2,1,0:T(8,128)(2,1)}, u32[]{:S(2)}, u32[]{:S(2)}) async-start(bf16[16,128,128]{2,1,0:T(8,128)(2,1)} %bitcast.202), calls=%async_computation.6 | async-start | bytes 1048576 | tf_op jit(solution)/shard_map/all_to_all | solution.py:151
  292.2 14.4 %all-to-all-start.5 = ((bf16[16,128,128]{2,1,0:T(8,128)(2,1)}), bf16[16,128,128]{2,1,0:T(8,128)(2,1)S(1)}, u32[]{:S(2)}, u32[]{:S(2)}) async-start(bf16[16,128,128]{2,1,0:T(8,128)(2,1)} %bitcast.46), calls=%async_computation.5 | async-start | bytes 1048576 | tf_op jit(solution)/shard_map/all_to_all | solution.py:150
  (32 other events, 36.7 us)
where the time goes:
time: 311 us; the launch traced here: 308 us
  local copies, waits for them, and re-layouts  98.6 us (32%)
  waiting for transfers between devices  88.5 us (28%)
  starting transfers between devices  47 us (15%)
  matrix products  31.9 us (10%)
  other arithmetic  28.1 us (9%)
  loops' own time  13 us (4%)
    while x96, local copies, waits for them, and re-layouts  33.9 us
    all_to_all x1, waiting for transfers between devices, on_device(): lax.all_to_all(query_grad, 'head', split_axis=0, concat_axis=1, tiled=True)  23.3 us
    ppermute x4, waiting for transfers between devices, shifted(): return lax.ppermute(block, axis, route)  22.5 us
    dynamic_slice x32, local copies, waits for them, and re-layouts, step_fn(): g_part = lax.dynamic_slice_in_dim(g_seg, first_row, tile_rows, 0)  16.1 us
    and x16, other arithmetic, allowed_mask(): return inside & active  13.7 us
    all_to_all x1, waiting for transfers between devices, on_device(): lax.all_to_all(query, 'head', split_axis=1, concat_axis=0, tiled=True)  13.5 us
    another operation x1, loops' own time, on_device(): lax.scan(step_fn, (zero_acc, zero_acc), tile_ids)  13 us
    dynamic_update_slice x16, local copies, waits for them, and re-layouts, on_device(): lax.scan(step_fn, (zero_acc, zero_acc), tile_ids)  11.2 us
  transfers between devices with their start and end apart: 11, of which 9 were waited for; matrix products, arithmetic and copies ran while one was open for 7% of the time, Pallas kernels for 0%

commit v1 on v0

v1 whole, which is shorter than its diff:
```python
import math

import jax
import jax.numpy as jnp
from jax import lax
from jax.experimental import pallas as pl
from jax.experimental.pallas import tpu as pltpu
from jax.sharding import PartitionSpec as P

HEAD_WIDTH = 128
BLOCK = 128
SPAN_BLOCKS = 9
CHUNK = 3
WINDOW = 1024
PRE_SCALE = 168.0 ** (-0.5)
EXP2_SCALE = PRE_SCALE / math.log(2.0)

F32 = jnp.float32
BF16 = jnp.bfloat16
MESH = pl.DeviceIdType.MESH

NT = (((1,), (1,)), ((), ()))
TN = (((0,), (0,)), ((), ()))
NN = (((1,), (0,)), ((), ()))


def dot(a, b, dims):
    return lax.dot_general(a, b, dims, preferred_element_type=F32)


def fold(x, op):
    return op(x.reshape(BLOCK // 8, 8, x.shape[1]), axis=0)


def bytes_of(ref, sem):
    return pltpu.make_async_copy(ref, ref, sem)


def block_grads(bits, first_row, q2, g2, kv, st, dp, pbs, dss, dk, dv):
    cols = q2.shape[0]
    u_index = lax.broadcasted_iota(jnp.int32, (BLOCK, cols), 0)
    t_index = lax.rem(lax.broadcasted_iota(jnp.int32, (BLOCK, cols), 1), BLOCK)
    causal = u_index <= t_index
    rows = CHUNK * BLOCK

    def span(c):
        return pl.ds(pl.multiple_of(first_row + c * rows, BLOCK), rows)

    m8 = jnp.full((8, cols), -jnp.inf, F32)
    for c in range(SPAN_BLOCKS // CHUNK):
        s = dot(kv[0, span(c), :], q2, NT)
        for i in range(CHUNK):
            o = c * CHUNK + i
            part = s[i * BLOCK : (i + 1) * BLOCK]
            if o == SPAN_BLOCKS - 1:
                part = jnp.where(causal, part, -jnp.inf)
            if o == 0:
                part = jnp.where(causal, -jnp.inf, part)
            st[o] = part
            m8 = jnp.maximum(m8, jnp.where(bits[o], fold(part, jnp.max), -jnp.inf))
    row_max = jnp.max(m8, axis=0, keepdims=True)

    l8 = jnp.zeros((8, cols), F32)
    d8 = jnp.zeros((8, cols), F32)
    for c in range(SPAN_BLOCKS // CHUNK):
        d = dot(kv[1, span(c), :], g2, NT)
        for i in range(CHUNK):
            o = c * CHUNK + i
            part = d[i * BLOCK : (i + 1) * BLOCK]
            shift = jnp.where(bits[o], row_max, jnp.inf)
            e = jnp.exp2((st[o] - shift) * EXP2_SCALE)
            st[o] = e
            dp[o] = part
            l8 += fold(e, jnp.sum)
            d8 += fold(e * part, jnp.sum)
    inverse = 1.0 / jnp.sum(l8, axis=0, keepdims=True)
    delta = jnp.sum(d8, axis=0, keepdims=True) * inverse

    dq = jnp.zeros((cols, HEAD_WIDTH), F32)
    for c in range(SPAN_BLOCKS // CHUNK):
        for i in range(CHUNK):
            o = c * CHUNK + i
            p = st[o] * inverse
            pbs[pl.ds(o * BLOCK, BLOCK), :] = p.astype(BF16)
            dss[pl.ds(o * BLOCK, BLOCK), :] = (p * (dp[o] - delta)).astype(BF16)
        pb = pbs[pl.ds(c * rows, rows), :]
        ds = dss[pl.ds(c * rows, rows), :]
        dv[span(c), :] += dot(pb, g2, NN)
        dk[span(c), :] += dot(ds, q2, NN)
        dq += dot(ds, kv[0, span(c), :], TN)
    return dq * PRE_SCALE


def kernel(
    n_z, q_ref, k_ref, v_ref, g_ref, mask_ref, dq_out, dk_out, dv_out,
    kv, qg, dqs, dkvs, halo_out, halo_in, dk, dv, st, dp, pbs, dss, bits_ref,
    s_q, s_g, s_k, s_v, r_qg, r_kv, s_halo, r_halo, s_back, r_back,
    s_dq, s_dk, s_dv, r_dq, r_dk, r_dv, m_sem,
):
    ctx = lax.axis_index("ctx")
    me_h = lax.axis_index("head")
    z, xh = lax.div(ctx, 2), lax.rem(ctx, 2)
    y, xl, core = lax.div(me_h, 4), lax.rem(lax.div(me_h, 2), 2), lax.rem(me_h, 2)
    x = xh * 2 + xl
    my_head = x * 4 + y
    seg = z * 2 + core
    n_blocks = qg.shape[0]
    half = n_blocks // 2
    other = me_h + 1 - 2 * core
    after = (lax.rem(z + core, n_z) * 2 + xh, other)
    before = (lax.rem(z + n_z - 1 + core, n_z) * 2 + xh, other)

    def target(i):
        pair, second = lax.div(i, 2), lax.rem(i, 2)
        dx, dy = lax.rem(pair, 2) + 2 * second, lax.div(pair, 2)
        tx, ty = lax.rem(x + dx, 4), lax.rem(y + dy, 4)
        return (z * 2 + lax.div(tx, 2), ty * 4 + lax.rem(tx, 2) * 2 + xh), tx * 4 + ty

    def source(i):
        pair, sc = lax.div(i, 2), lax.rem(i, 2)
        dx, dy = lax.rem(pair, 2), lax.div(pair, 2)
        return lax.rem(y + 4 - dy, 4) * 4 + lax.rem(x + dx, 2) * 2 + sc

    rows_mask = pltpu.make_async_copy(
        mask_ref.at[pl.ds(pl.multiple_of(seg * n_blocks, 8), n_blocks), :], bits_ref, m_sem
    )
    rows_mask.start()

    barrier = pltpu.get_barrier_semaphore()

    def greet(i, carry):
        device, _ = target(i)
        pl.semaphore_signal(barrier, inc=1, device_id=device, device_id_type=MESH)
        pl.semaphore_signal(barrier, inc=1, device_id=(seg, i), device_id_type=MESH)
        return carry

    lax.fori_loop(0, n_blocks, greet, 0)
    pl.semaphore_signal(barrier, inc=1, device_id=after, device_id_type=MESH)
    pl.semaphore_signal(barrier, inc=1, device_id=before, device_id_type=MESH)
    pl.semaphore_wait(barrier, 2 * n_blocks + 2)

    mine = xh == core

    def send(is_self, device, src, dst, send_sem, recv_sem):
        @pl.when(is_self)
        def _():
            pltpu.make_async_copy(src, dst, recv_sem).start()

        @pl.when(jnp.logical_not(is_self))
        def _():
            pltpu.make_async_remote_copy(
                src_ref=src, dst_ref=dst, send_sem=send_sem, recv_sem=recv_sem,
                device_id=device, device_id_type=MESH,
            ).start()

    key_rows = pl.ds(pl.multiple_of(WINDOW + me_h * BLOCK, BLOCK), BLOCK)

    def send_kv(i, carry):
        device, head = target(i)
        is_self = jnp.logical_and(mine, i == 0)
        cols = pl.ds(pl.multiple_of(head * HEAD_WIDTH, HEAD_WIDTH), HEAD_WIDTH)
        send(is_self, device, k_ref.at[:, cols], kv.at[0, key_rows, :], s_k, r_kv.at[me_h])
        send(is_self, device, v_ref.at[:, cols], kv.at[1, key_rows, :], s_v, r_kv.at[me_h])
        return carry

    def send_qg(i, carry):
        device, head = target(i)
        is_self = jnp.logical_and(mine, i == 0)
        cols = pl.ds(pl.multiple_of(head * 2 * HEAD_WIDTH, 2 * HEAD_WIDTH), 2 * HEAD_WIDTH)
        send(is_self, device, q_ref.at[:, cols], qg.at[me_h, 0], s_q, r_qg.at[me_h])
        send(is_self, device, g_ref.at[:, cols], qg.at[me_h, 1], s_g, r_qg.at[me_h])
        return carry

    lax.fori_loop(0, n_blocks, send_kv, 0)
    lax.fori_loop(0, n_blocks, send_qg, 0)

    dk[...] = jnp.zeros_like(dk)
    dv[...] = jnp.zeros_like(dv)

    def take_kv(i, carry):
        h = source(i)
        rows = pl.ds(pl.multiple_of(WINDOW + h * BLOCK, BLOCK), BLOCK)
        bytes_of(kv.at[:, rows, :], r_kv.at[h]).wait()

        @pl.when(h >= half)
        def _():
            lead = pl.ds(pl.multiple_of((h - half) * BLOCK, BLOCK), BLOCK)
            pltpu.make_async_remote_copy(
                src_ref=kv.at[:, rows, :], dst_ref=kv.at[:, lead, :], send_sem=s_halo,
                recv_sem=r_halo, device_id=after, device_id_type=MESH,
            ).start()

        return carry

    lax.fori_loop(0, n_blocks, take_kv, 0)
    rows_mask.wait()
    bytes_of(kv.at[:, pl.ds(0, WINDOW), :], r_halo).wait()

    head_cols = pl.ds(pl.multiple_of(my_head * HEAD_WIDTH, HEAD_WIDTH), HEAD_WIDTH)
    pair_cols = pl.ds(pl.multiple_of(my_head * 2 * HEAD_WIDTH, 2 * HEAD_WIDTH), 2 * HEAD_WIDTH)

    def work(i, carry):
        h = source(i)
        bytes_of(qg.at[h], r_qg.at[h]).wait()
        bits = [
            (bits_ref[h, SPAN_BLOCKS - 1 - o] > 0) & (seg * n_blocks + h + o >= SPAN_BLOCKS - 1)
            for o in range(SPAN_BLOCKS)
        ]
        q2 = jnp.concatenate([qg[h, 0, :, :HEAD_WIDTH], qg[h, 0, :, HEAD_WIDTH:]], axis=0)
        g2 = jnp.concatenate([qg[h, 1, :, :HEAD_WIDTH], qg[h, 1, :, HEAD_WIDTH:]], axis=0)
        dq = block_grads(bits, h * BLOCK, q2, g2, kv, st, dp, pbs, dss, dk, dv)
        dqs[h] = jnp.concatenate([dq[:BLOCK], dq[BLOCK:]], axis=1).astype(BF16)
        is_self = jnp.logical_and(mine, h == me_h)
        send(is_self, (seg, h), dqs.at[h], dq_out.at[:, pair_cols], s_dq, r_dq)
        return carry

    lax.fori_loop(0, n_blocks, work, 0)

    halo_out[0] = (dk[pl.ds(0, WINDOW), :] * PRE_SCALE).astype(BF16)
    halo_out[1] = dv[pl.ds(0, WINDOW), :].astype(BF16)
    back = pltpu.make_async_remote_copy(
        src_ref=halo_out, dst_ref=halo_in, send_sem=s_back, recv_sem=r_back,
        device_id=before, device_id_type=MESH,
    )
    back.start()

    def send_dkv(h):
        is_self = jnp.logical_and(mine, h == me_h)
        send(is_self, (seg, h), dkvs.at[0, h], dk_out.at[:, head_cols], s_dk, r_dk)
        send(is_self, (seg, h), dkvs.at[1, h], dv_out.at[:, head_cols], s_dv, r_dv)

    def finish_low(h, carry):
        rows = pl.ds(pl.multiple_of(WINDOW + h * BLOCK, BLOCK), BLOCK)
        dkvs[0, h] = (dk[rows, :] * PRE_SCALE).astype(BF16)
        dkvs[1, h] = dv[rows, :].astype(BF16)
        send_dkv(h)
        return carry

    lax.fori_loop(0, half, finish_low, 0)
    back.wait_recv()

    def finish_high(h, carry):
        rows = pl.ds(pl.multiple_of(WINDOW + h * BLOCK, BLOCK), BLOCK)
        lead = pl.ds(pl.multiple_of((h - half) * BLOCK, BLOCK), BLOCK)
        dkvs[0, h] = (dk[rows, :] * PRE_SCALE + halo_in[0, lead, :].astype(F32)).astype(BF16)
        dkvs[1, h] = (dv[rows, :] + halo_in[1, lead, :].astype(F32)).astype(BF16)
        send_dkv(h)
        return carry

    lax.fori_loop(half, n_blocks, finish_high, 0)

    back.wait_send()
    bytes_of(kv.at[:, pl.ds(0, WINDOW), :], s_halo).wait()

    def sent(ref, width, sem):
        @pl.when(mine)
        def _():
            bytes_of(ref.at[:, pl.ds(0, (n_blocks - 1) * width)], sem).wait()

        @pl.when(jnp.logical_not(mine))
        def _():
            bytes_of(ref, sem).wait()

    for ref, width, sem in (
        (q_ref, 2 * HEAD_WIDTH, s_q),
        (g_ref, 2 * HEAD_WIDTH, s_g),
        (k_ref, HEAD_WIDTH, s_k),
        (v_ref, HEAD_WIDTH, s_v),
        (dq_out, 2 * HEAD_WIDTH, s_dq),
        (dk_out, HEAD_WIDTH, s_dk),
        (dv_out, HEAD_WIDTH, s_dv),
    ):
        sent(ref, width, sem)
    bytes_of(dq_out, r_dq).wait()
    bytes_of(dk_out, r_dk).wait()
    bytes_of(dv_out, r_dv).wait()


def solution(mesh):
    n_z = mesh.shape["ctx"] // 2
    n_blocks = mesh.shape["head"]

    def on_device(query, key, value, out_grad, block_mask):
        any_space = pl.BlockSpec(memory_space=pl.ANY)
        dma = pltpu.SemaphoreType.DMA
        keys = n_blocks * BLOCK + WINDOW
        cols = 2 * BLOCK

        def body(*refs):
            kernel(n_z, *refs)

        return pl.pallas_call(
            body,
            out_shape=(
                jax.ShapeDtypeStruct(query.shape, BF16),
                jax.ShapeDtypeStruct(key.shape, BF16),
                jax.ShapeDtypeStruct(value.shape, BF16),
            ),
            in_specs=[any_space] * 5,
            out_specs=(any_space,) * 3,
            scratch_shapes=[
                pltpu.VMEM((2, keys, HEAD_WIDTH), BF16),
                pltpu.VMEM((n_blocks, 2, BLOCK, 2 * HEAD_WIDTH), BF16),
                pltpu.VMEM((n_blocks, BLOCK, 2 * HEAD_WIDTH), BF16),
                pltpu.VMEM((2, n_blocks, BLOCK, HEAD_WIDTH), BF16),
                pltpu.VMEM((2, WINDOW, HEAD_WIDTH), BF16),
                pltpu.VMEM((2, WINDOW, HEAD_WIDTH), BF16),
                pltpu.VMEM((keys, HEAD_WIDTH), F32),
                pltpu.VMEM((keys, HEAD_WIDTH), F32),
                pltpu.VMEM((SPAN_BLOCKS, BLOCK, cols), F32),
                pltpu.VMEM((SPAN_BLOCKS, BLOCK, cols), F32),
                pltpu.VMEM((SPAN_BLOCKS * BLOCK, cols), BF16),
                pltpu.VMEM((SPAN_BLOCKS * BLOCK, cols), BF16),
                pltpu.SMEM((n_blocks, block_mask.shape[1]), jnp.int32),
                dma, dma, dma, dma, dma((n_blocks,)), dma((n_blocks,)),
                dma, dma, dma, dma, dma, dma, dma, dma, dma, dma, dma,
            ],
            compiler_params=pltpu.CompilerParams(collective_id=0, has_side_effects=True),
            name="window_attention_grads",
        )(query, key, value, out_grad, block_mask)

    tokens = P(("ctx", "head"), None)
    return jax.shard_map(
        on_device,
        mesh=mesh,
        in_specs=(tokens, tokens, tokens, tokens, P()),
        out_specs=(tokens, tokens, tokens),
        check_vma=False,
    )
```

time: 311 us -> 88 us (0.28)
  the two profiles are of different devices: /device:TPU:1 before, /device:TPU:153 now
where the time goes in v1:
time: 88 us; the launch traced here: 87.7 us
  Pallas kernels  81.1 us (92%)
  local copies, waits for them, and re-layouts  5.98 us (7%)
    pallas_call x1, Pallas kernels, on_device(): pl.pallas_call(body, out_shape=(jax.ShapeDtypeStruct(query.shape, BF16),...  81.1 us
    unnamed x8, local copies, waits for them, and re-layouts  5.98 us

profile of v1, /device:TPU:153, one launch (start us, length us, event | category | flops | bytes accessed | tf_op | source)
XLA Modules:
  0.0 87.7 jit_solution(2555064164495181422)
XLA Ops:
  0.6 1.6 %copy.8.refs_4_ = s32[512,9]{1,0:T(8,128)} copy(s32[512,9]{0,1:T(8,128)} %param.9) | data formatting | bytes 36864 | tf_op args[4]
  2.2 81.1 %window_attention_grads.1 = (bf16[128,4096]{1,0:T(8,128)(2,1)}, bf16[128,2048]{1,0:T(8,128)(2,1)}, bf16[128,2048]{1,0:T(8,128)(2,1)}) custom-call(bf16[128,4096]{1,0:T(8,128)(2,1)} %refs_0_.1, bf16[128,2048]{1,0:T(8,128)(2,1)} %refs_1_.1, bf16[128,2048]{1,0:T(8,128)(2,1)} %refs_2_.1, bf16[128,4096]{1,0:T(8,128)(2,1)} %refs_3_.1, s32[512,9]{1,0:T(8,128)} %copy.8.refs_4_), custom_call_target="tpu_custom_call" | custom-call | tf_op jit(solution)/shard_map/window_attention_grads/pallas_call | solution.py:292
  83.3 0.0 copy-start.1
  83.4 2.3 %copy.12 = bf16[128,4096]{1,0:T(8,128)(2,1)} copy(bf16[128,4096]{1,0:T(8,128)(2,1)} %get-tuple-element.6) | data formatting | bytes 2097152
  85.7 0.0 copy-done.1
  85.7 0.0 copy-start
  85.7 0.8 copy.13
  86.5 0.4 copy-done
  86.9 0.8 copy.14
Async XLA Ops:
  83.3 2.4 %copy-start.1 = (bf16[128,2048]{1,0:T(8,128)(2,1)S(1)}, bf16[128,2048]{1,0:T(8,128)(2,1)}, u32[]{:S(2)}) copy-start(bf16[128,2048]{1,0:T(8,128)(2,1)} %get-tuple-element.7) | copy-start | bytes 1572868
  85.7 1.2 %copy-start = (bf16[128,2048]{1,0:T(8,128)(2,1)S(1)}, bf16[128,2048]{1,0:T(8,128)(2,1)}, u32[]{:S(2)}) copy-start(bf16[128,2048]{1,0:T(8,128)(2,1)} %get-tuple-element.8) | copy-start | bytes 1572868

commit v2 on v1

--- a/solution.py
+++ b/solution.py
@@ -9,6 +9,7 @@
 
 HEAD_WIDTH = 128
 BLOCK = 128
+LANES = 128
 SPAN_BLOCKS = 9
 CHUNK = 3
 WINDOW = 1024
@@ -110,20 +111,28 @@
     after = (lax.rem(z + core, n_z) * 2 + xh, other)
     before = (lax.rem(z + n_z - 1 + core, n_z) * 2 + xh, other)
 
+    way = 1 - 2 * core
+
+    def pair_step(pair):
+        dx = lax.rem(pair, 2)
+        return dx, lax.rem(lax.div(pair, 2) + 2 * dx, 4)
+
     def target(i):
         pair, second = lax.div(i, 2), lax.rem(i, 2)
-        dx, dy = lax.rem(pair, 2) + 2 * second, lax.div(pair, 2)
-        tx, ty = lax.rem(x + dx, 4), lax.rem(y + dy, 4)
+        dx, dy = pair_step(pair)
+        dx = dx + 2 * second
+        tx, ty = lax.rem(x + 4 + way * dx, 4), lax.rem(y + 4 + way * dy, 4)
         return (z * 2 + lax.div(tx, 2), ty * 4 + lax.rem(tx, 2) * 2 + xh), tx * 4 + ty
 
     def source(i):
         pair, sc = lax.div(i, 2), lax.rem(i, 2)
-        dx, dy = lax.rem(pair, 2), lax.div(pair, 2)
-        return lax.rem(y + 4 - dy, 4) * 4 + lax.rem(x + dx, 2) * 2 + sc
-
-    rows_mask = pltpu.make_async_copy(
-        mask_ref.at[pl.ds(pl.multiple_of(seg * n_blocks, 8), n_blocks), :], bits_ref, m_sem
-    )
+        dx, dy = pair_step(pair)
+        return lax.rem(y + 4 - (1 - 2 * sc) * dy, 4) * 4 + lax.rem(x + dx, 2) * 2 + sc
+
+    lanes = bits_ref.shape[1]
+    seg_lane = lax.rem(seg * n_blocks, lanes)
+    lane_tile = pl.ds(pl.multiple_of(lax.div(seg * n_blocks, lanes) * lanes, lanes), lanes)
+    rows_mask = pltpu.make_async_copy(mask_ref.at[:, lane_tile], bits_ref, m_sem)
     rows_mask.start()
 
     barrier = pltpu.get_barrier_semaphore()
@@ -157,7 +166,7 @@
 
     def send_kv(i, carry):
         device, head = target(i)
-        is_self = jnp.logical_and(mine, i == 0)
+        is_self = jnp.logical_and(mine, head == my_head)
         cols = pl.ds(pl.multiple_of(head * HEAD_WIDTH, HEAD_WIDTH), HEAD_WIDTH)
         send(is_self, device, k_ref.at[:, cols], kv.at[0, key_rows, :], s_k, r_kv.at[me_h])
         send(is_self, device, v_ref.at[:, cols], kv.at[1, key_rows, :], s_v, r_kv.at[me_h])
@@ -165,7 +174,7 @@
 
     def send_qg(i, carry):
         device, head = target(i)
-        is_self = jnp.logical_and(mine, i == 0)
+        is_self = jnp.logical_and(mine, head == my_head)
         cols = pl.ds(pl.multiple_of(head * 2 * HEAD_WIDTH, 2 * HEAD_WIDTH), 2 * HEAD_WIDTH)
         send(is_self, device, q_ref.at[:, cols], qg.at[me_h, 0], s_q, r_qg.at[me_h])
         send(is_self, device, g_ref.at[:, cols], qg.at[me_h, 1], s_g, r_qg.at[me_h])
@@ -203,7 +212,7 @@
         h = source(i)
         bytes_of(qg.at[h], r_qg.at[h]).wait()
         bits = [
-            (bits_ref[h, SPAN_BLOCKS - 1 - o] > 0) & (seg * n_blocks + h + o >= SPAN_BLOCKS - 1)
+            (bits_ref[SPAN_BLOCKS - 1 - o, seg_lane + h] > 0) & (seg * n_blocks + h + o >= SPAN_BLOCKS - 1)
             for o in range(SPAN_BLOCKS)
         ]
         q2 = jnp.concatenate([qg[h, 0, :, :HEAD_WIDTH], qg[h, 0, :, HEAD_WIDTH:]], axis=0)
@@ -276,6 +285,17 @@
     bytes_of(dv_out, r_dv).wait()
 
 
+def put_out(a, b, c, a_out, b_out, c_out, a_sem, b_sem, c_sem):
+    copies = [
+        pltpu.make_async_copy(src, dst, sem)
+        for src, dst, sem in ((a, a_out, a_sem), (b, b_out, b_sem), (c, c_out, c_sem))
+    ]
+    for copy in copies:
+        copy.start()
+    for copy in copies:
+        copy.wait()
+
+
 def solution(mesh):
     n_z = mesh.shape["ctx"] // 2
     n_blocks = mesh.shape["head"]
@@ -289,7 +309,7 @@
         def body(*refs):
             kernel(n_z, *refs)
 
-        return pl.pallas_call(
+        landed = pl.pallas_call(
             body,
             out_shape=(
                 jax.ShapeDtypeStruct(query.shape, BF16),
@@ -311,13 +331,21 @@
                 pltpu.VMEM((SPAN_BLOCKS, BLOCK, cols), F32),
                 pltpu.VMEM((SPAN_BLOCKS * BLOCK, cols), BF16),
                 pltpu.VMEM((SPAN_BLOCKS * BLOCK, cols), BF16),
-                pltpu.SMEM((n_blocks, block_mask.shape[1]), jnp.int32),
+                pltpu.SMEM((block_mask.shape[1], LANES), jnp.int32),
                 dma, dma, dma, dma, dma((n_blocks,)), dma((n_blocks,)),
                 dma, dma, dma, dma, dma, dma, dma, dma, dma, dma, dma,
             ],
             compiler_params=pltpu.CompilerParams(collective_id=0, has_side_effects=True),
             name="window_attention_grads",
-        )(query, key, value, out_grad, block_mask)
+        )(query, key, value, out_grad, block_mask.T)
+        return pl.pallas_call(
+            put_out,
+            out_shape=tuple(jax.ShapeDtypeStruct(a.shape, BF16) for a in (query, key, value)),
+            in_specs=[pl.BlockSpec(memory_space=pltpu.VMEM)] * 3,
+            out_specs=(any_space,) * 3,
+            scratch_shapes=[dma, dma, dma],
+            name="put_out",
+        )(*landed)
 
     tokens = P(("ctx", "head"), None)
     return jax.shard_map(

time: 88 us -> 78.4 us (0.89)
  the two profiles are of different devices: /device:TPU:153 before, /device:TPU:1 now
where the time goes in v2:
time: 78.4 us; the launch traced here: 77.3 us
  Pallas kernels  76.7 us (98%)
    pallas_call x1, Pallas kernels, on_device(): pl.pallas_call(body, out_shape=(jax.ShapeDtypeStruct(query.shape, BF16),...  73.8 us
    pallas_call x1, Pallas kernels, on_device(): pl.pallas_call(put_out, out_shape=tuple((jax.ShapeDtypeStruct(a.shape, BF...  2.85 us

profile of v2, /device:TPU:1, one launch (start us, length us, event | category | flops | bytes accessed | tf_op | source)
XLA Modules:
  0.0 77.3 jit_solution(16097758710790434032)
XLA Ops:
  0.6 73.8 %window_attention_grads.1 = (bf16[128,4096]{1,0:T(8,128)(2,1)}, bf16[128,2048]{1,0:T(8,128)(2,1)}, bf16[128,2048]{1,0:T(8,128)(2,1)}) custom-call(bf16[128,4096]{1,0:T(8,128)(2,1)} %refs_0_.1, bf16[128,2048]{1,0:T(8,128)(2,1)} %refs_1_.1, bf16[128,2048]{1,0:T(8,128)(2,1)} %refs_2_.1, bf16[128,4096]{1,0:T(8,128)(2,1)} %refs_3_.1, s32[9,512]{1,0:T(8,128)} %bitcast.1), custom_call_target="tpu_custom_call" | custom-call | tf_op jit(solution)/shard_map/window_attention_grads/pallas_call | solution.py:312
  74.5 2.9 %put_out.1 = (bf16[128,4096]{1,0:T(8,128)(2,1)}, bf16[128,2048]{1,0:T(8,128)(2,1)}, bf16[128,2048]{1,0:T(8,128)(2,1)}) custom-call(bf16[128,4096]{1,0:T(8,128)(2,1)} %get-tuple-element.6.a, bf16[128,2048]{1,0:T(8,128)(2,1)} %get-tuple-element.7.b, bf16[128,2048]{1,0:T(8,128)(2,1)} %get-tuple-element.8.c), custom_call_target="tpu_custom_call" | custom-call | tf_op jit(solution)/shard_map/put_out/pallas_call | solution.py:341

commit v3 on v2

--- a/solution.py
+++ b/solution.py
@@ -312,12 +312,12 @@
         landed = pl.pallas_call(
             body,
             out_shape=(
-                jax.ShapeDtypeStruct(query.shape, BF16),
-                jax.ShapeDtypeStruct(key.shape, BF16),
-                jax.ShapeDtypeStruct(value.shape, BF16),
+                pltpu.VMEM(query.shape, BF16),
+                pltpu.VMEM(key.shape, BF16),
+                pltpu.VMEM(value.shape, BF16),
             ),
             in_specs=[any_space] * 5,
-            out_specs=(any_space,) * 3,
+            out_specs=(pl.BlockSpec(memory_space=pltpu.VMEM),) * 3,
             scratch_shapes=[
                 pltpu.VMEM((2, keys, HEAD_WIDTH), BF16),
                 pltpu.VMEM((n_blocks, 2, BLOCK, 2 * HEAD_WIDTH), BF16),
@@ -341,10 +341,11 @@
         return pl.pallas_call(
             put_out,
             out_shape=tuple(jax.ShapeDtypeStruct(a.shape, BF16) for a in (query, key, value)),
-            in_specs=[pl.BlockSpec(memory_space=pltpu.VMEM)] * 3,
+            in_specs=[any_space] * 3,
             out_specs=(any_space,) * 3,
             scratch_shapes=[dma, dma, dma],
             name="put_out",
+            compiler_params=pltpu.CompilerParams(vmem_limit_bytes=2**20),
         )(*landed)
 
     tokens = P(("ctx", "head"), None)

time: 78.4 us -> 76.6 us (0.977)
  Pallas kernels: 76.7 us -> 75 us
    pallas_call x1, Pallas kernels: 2.85 us -> 1.34 us  [on_device(): pl.pallas_call(put_out, out_shape=tuple((jax.ShapeDtypeStruct(a.shape, BF...]
where the time goes in v3:
time: 76.6 us; the launch traced here: 75.7 us
  Pallas kernels  75 us (98%)
    pallas_call x1, Pallas kernels, on_device(): pl.pallas_call(body, out_shape=(pltpu.VMEM(query.shape, BF16), pltpu.VMEM...  73.7 us

profile of v3, /device:TPU:1, one launch (start us, length us, event | category | flops | bytes accessed | tf_op | source)
XLA Modules:
  0.0 75.7 jit_solution(2983247813266769726)
XLA Ops:
  0.6 73.7 %window_attention_grads.1 = (bf16[128,4096]{1,0:T(8,128)(2,1)S(1)}, bf16[128,2048]{1,0:T(8,128)(2,1)S(1)}, bf16[128,2048]{1,0:T(8,128)(2,1)S(1)}) custom-call(bf16[128,4096]{1,0:T(8,128)(2,1)} %refs_0_.1, bf16[128,2048]{1,0:T(8,128)(2,1)} %refs_1_.1, bf16[128,2048]{1,0:T(8,128)(2,1)} %refs_2_.1, bf16[128,4096]{1,0:T(8,128)(2,1)} %refs_3_.1, s32[9,512]{1,0:T(8,128)} %bitcast.1), custom_call_target="tpu_custom_call" | custom-call | tf_op jit(solution)/shard_map/window_attention_grads/pallas_call | solution.py:312
  74.3 1.3 %put_out.1 = (bf16[128,4096]{1,0:T(8,128)(2,1)}, bf16[128,2048]{1,0:T(8,128)(2,1)}, bf16[128,2048]{1,0:T(8,128)(2,1)}) custom-call(bf16[128,4096]{1,0:T(8,128)(2,1)S(1)} %get-tuple-element.6.a, bf16[128,2048]{1,0:T(8,128)(2,1)S(1)} %get-tuple-element.7.b, bf16[128,2048]{1,0:T(8,128)(2,1)S(1)} %get-tuple-element.8.c), custom_call_target="tpu_custom_call" | custom-call | tf_op jit(solution)/shard_map/put_out/pallas_call | solution.py:341

commit v4 on v3

--- a/solution.py
+++ b/solution.py
@@ -96,7 +96,7 @@
     n_z, q_ref, k_ref, v_ref, g_ref, mask_ref, dq_out, dk_out, dv_out,
     kv, qg, dqs, dkvs, halo_out, halo_in, dk, dv, st, dp, pbs, dss, bits_ref,
     s_q, s_g, s_k, s_v, r_qg, r_kv, s_halo, r_halo, s_back, r_back,
-    s_dq, s_dk, s_dv, r_dq, r_dk, r_dv, m_sem,
+    s_dq, s_dk, s_dv, r_dq, r_dk, r_dv, m_sem, peer_sem,
 ):
     ctx = lax.axis_index("ctx")
     me_h = lax.axis_index("head")
@@ -138,15 +138,25 @@
     barrier = pltpu.get_barrier_semaphore()
 
     def greet(i, carry):
-        device, _ = target(i)
-        pl.semaphore_signal(barrier, inc=1, device_id=device, device_id_type=MESH)
-        pl.semaphore_signal(barrier, inc=1, device_id=(seg, i), device_id_type=MESH)
+        chip = (z * 2 + lax.div(i, 8), lax.rem(i, 8) * 2)
+        pl.semaphore_signal(barrier, inc=1, device_id=chip, device_id_type=MESH)
         return carry
 
     lax.fori_loop(0, n_blocks, greet, 0)
-    pl.semaphore_signal(barrier, inc=1, device_id=after, device_id_type=MESH)
-    pl.semaphore_signal(barrier, inc=1, device_id=before, device_id_type=MESH)
-    pl.semaphore_wait(barrier, 2 * n_blocks + 2)
+    beyond = (lax.rem(z + n_z - 1 + 2 * core, n_z) * 2 + xh, me_h - core + 1)
+    pl.semaphore_signal(barrier, inc=1, device_id=beyond, device_id_type=MESH)
+
+    def tell_other_core():
+        pl.semaphore_signal(peer_sem, inc=1, device_id=(ctx, other), device_id_type=MESH)
+
+    @pl.when(core == 0)
+    def _():
+        pl.semaphore_wait(barrier, 2 * n_blocks)
+        tell_other_core()
+
+    @pl.when(core == 1)
+    def _():
+        pl.semaphore_wait(peer_sem, 1)
 
     mine = xh == core
 
@@ -185,6 +195,11 @@
 
     dk[...] = jnp.zeros_like(dk)
     dv[...] = jnp.zeros_like(dv)
+
+    @pl.when(core == 1)
+    def _():
+        pl.semaphore_wait(barrier, 2)
+        tell_other_core()
 
     def take_kv(i, carry):
         h = source(i)
@@ -231,6 +246,11 @@
         src_ref=halo_out, dst_ref=halo_in, send_sem=s_back, recv_sem=r_back,
         device_id=before, device_id_type=MESH,
     )
+
+    @pl.when(core == 0)
+    def _():
+        pl.semaphore_wait(peer_sem, 1)
+
     back.start()
 
     def send_dkv(h):
@@ -334,6 +354,7 @@
                 pltpu.SMEM((block_mask.shape[1], LANES), jnp.int32),
                 dma, dma, dma, dma, dma((n_blocks,)), dma((n_blocks,)),
                 dma, dma, dma, dma, dma, dma, dma, dma, dma, dma, dma,
+                pltpu.SemaphoreType.REGULAR,
             ],
             compiler_params=pltpu.CompilerParams(collective_id=0, has_side_effects=True),
             name="window_attention_grads",

time: 76.6 us -> 76.8 us (level)
  Pallas kernels: 75 us -> 76 us
    pallas_call x1, Pallas kernels: 73.7 us -> 74.7 us  [on_device(): pl.pallas_call(body, out_shape=(pltpu.VMEM(query.shape, BF16), pltpu.VMEM...]
where the time goes in v4:
time: 76.8 us; the launch traced here: 76.7 us
  Pallas kernels  76 us (99%)
    pallas_call x1, Pallas kernels, on_device(): pl.pallas_call(body, out_shape=(pltpu.VMEM(query.shape, BF16), pltpu.VMEM...  74.7 us

profile of v4, /device:TPU:1, one launch (start us, length us, event | category | flops | bytes accessed | tf_op | source)
XLA Modules:
  0.0 76.7 jit_solution(6270243969548345000)
XLA Ops:
  0.6 74.7 %window_attention_grads.1 = (bf16[128,4096]{1,0:T(8,128)(2,1)S(1)}, bf16[128,2048]{1,0:T(8,128)(2,1)S(1)}, bf16[128,2048]{1,0:T(8,128)(2,1)S(1)}) custom-call(bf16[128,4096]{1,0:T(8,128)(2,1)} %refs_0_.1, bf16[128,2048]{1,0:T(8,128)(2,1)} %refs_1_.1, bf16[128,2048]{1,0:T(8,128)(2,1)} %refs_2_.1, bf16[128,4096]{1,0:T(8,128)(2,1)} %refs_3_.1, s32[9,512]{1,0:T(8,128)} %bitcast.1), custom_call_target="tpu_custom_call" | custom-call | tf_op jit(solution)/shard_map/window_attention_grads/pallas_call | solution.py:332
  75.3 1.3 %put_out.1 = (bf16[128,4096]{1,0:T(8,128)(2,1)}, bf16[128,2048]{1,0:T(8,128)(2,1)}, bf16[128,2048]{1,0:T(8,128)(2,1)}) custom-call(bf16[128,4096]{1,0:T(8,128)(2,1)S(1)} %get-tuple-element.6.a, bf16[128,2048]{1,0:T(8,128)(2,1)S(1)} %get-tuple-element.7.b, bf16[128,2048]{1,0:T(8,128)(2,1)S(1)} %get-tuple-element.8.c), custom_call_target="tpu_custom_call" | custom-call | tf_op jit(solution)/shard_map/put_out/pallas_call | solution.py:362

commit v5 on v4

--- a/solution.py
+++ b/solution.py
@@ -223,8 +223,31 @@
     head_cols = pl.ds(pl.multiple_of(my_head * HEAD_WIDTH, HEAD_WIDTH), HEAD_WIDTH)
     pair_cols = pl.ds(pl.multiple_of(my_head * 2 * HEAD_WIDTH, 2 * HEAD_WIDTH), 2 * HEAD_WIDTH)
 
+    back = pltpu.make_async_remote_copy(
+        src_ref=halo_out, dst_ref=halo_in, send_sem=s_back, recv_sem=r_back,
+        device_id=before, device_id_type=MESH,
+    )
+
+    def send_back():
+        halo_out[0] = (dk[pl.ds(0, WINDOW), :] * PRE_SCALE).astype(BF16)
+        halo_out[1] = dv[pl.ds(0, WINDOW), :].astype(BF16)
+
+        @pl.when(core == 0)
+        def _():
+            pl.semaphore_wait(peer_sem, 1)
+
+        back.start()
+
+    last = n_blocks - 4
+
+    def turn(i):
+        m = lax.rem(i + 2 * lax.rem(lax.div(y + 1, 2), 2), 4)
+        swapped = last + lax.div(m, 2) + lax.rem(m, 2) * (3 - 2 * lax.div(m, 2))
+        return i + lax.div(i, last) * (swapped - i)
+
     def work(i, carry):
-        h = source(i)
+        pl.when(i == n_blocks - 2)(send_back)
+        h = source(turn(i))
         bytes_of(qg.at[h], r_qg.at[h]).wait()
         bits = [
             (bits_ref[SPAN_BLOCKS - 1 - o, seg_lane + h] > 0) & (seg * n_blocks + h + o >= SPAN_BLOCKS - 1)
@@ -239,19 +262,6 @@
         return carry
 
     lax.fori_loop(0, n_blocks, work, 0)
-
-    halo_out[0] = (dk[pl.ds(0, WINDOW), :] * PRE_SCALE).astype(BF16)
-    halo_out[1] = dv[pl.ds(0, WINDOW), :].astype(BF16)
-    back = pltpu.make_async_remote_copy(
-        src_ref=halo_out, dst_ref=halo_in, send_sem=s_back, recv_sem=r_back,
-        device_id=before, device_id_type=MESH,
-    )
-
-    @pl.when(core == 0)
-    def _():
-        pl.semaphore_wait(peer_sem, 1)
-
-    back.start()
 
     def send_dkv(h):
         is_self = jnp.logical_and(mine, h == me_h)

time: 76.8 us -> 75.8 us (0.987)
  Pallas kernels: 76 us -> 75 us
    pallas_call x1, Pallas kernels: 74.7 us -> 73.7 us  [on_device(): pl.pallas_call(body, out_shape=(pltpu.VMEM(query.shape, BF16), pltpu.VMEM...]
where the time goes in v5:
time: 75.8 us; the launch traced here: 75.6 us
  Pallas kernels  75 us (99%)
    pallas_call x1, Pallas kernels, on_device(): pl.pallas_call(body, out_shape=(pltpu.VMEM(query.shape, BF16), pltpu.VMEM...  73.7 us

profile of v5, /device:TPU:1, one launch (start us, length us, event | category | flops | bytes accessed | tf_op | source)
XLA Modules:
  0.0 75.6 jit_solution(17834067458713233644)
XLA Ops:
  0.6 73.7 %window_attention_grads.1 = (bf16[128,4096]{1,0:T(8,128)(2,1)S(1)}, bf16[128,2048]{1,0:T(8,128)(2,1)S(1)}, bf16[128,2048]{1,0:T(8,128)(2,1)S(1)}) custom-call(bf16[128,4096]{1,0:T(8,128)(2,1)} %refs_0_.1, bf16[128,2048]{1,0:T(8,128)(2,1)} %refs_1_.1, bf16[128,2048]{1,0:T(8,128)(2,1)} %refs_2_.1, bf16[128,4096]{1,0:T(8,128)(2,1)} %refs_3_.1, s32[9,512]{1,0:T(8,128)} %bitcast.1), custom_call_target="tpu_custom_call" | custom-call | tf_op jit(solution)/shard_map/window_attention_grads/pallas_call | solution.py:342
  74.3 1.3 %put_out.1 = (bf16[128,4096]{1,0:T(8,128)(2,1)}, bf16[128,2048]{1,0:T(8,128)(2,1)}, bf16[128,2048]{1,0:T(8,128)(2,1)}) custom-call(bf16[128,4096]{1,0:T(8,128)(2,1)S(1)} %get-tuple-element.6.a, bf16[128,2048]{1,0:T(8,128)(2,1)S(1)} %get-tuple-element.7.b, bf16[128,2048]{1,0:T(8,128)(2,1)S(1)} %get-tuple-element.8.c), custom_call_target="tpu_custom_call" | custom-call | tf_op jit(solution)/shard_map/put_out/pallas_call | solution.py:372

commit v6 on v5

--- a/solution.py
+++ b/solution.py
@@ -218,7 +218,6 @@
 
     lax.fori_loop(0, n_blocks, take_kv, 0)
     rows_mask.wait()
-    bytes_of(kv.at[:, pl.ds(0, WINDOW), :], r_halo).wait()
 
     head_cols = pl.ds(pl.multiple_of(my_head * HEAD_WIDTH, HEAD_WIDTH), HEAD_WIDTH)
     pair_cols = pl.ds(pl.multiple_of(my_head * 2 * HEAD_WIDTH, 2 * HEAD_WIDTH), 2 * HEAD_WIDTH)
@@ -241,11 +240,17 @@
     last = n_blocks - 4
 
     def turn(i):
+        first = lax.rem(i + 2 * (1 - lax.div(y, 2)), 4)
+        early = lax.div(n_blocks + 3 - i, n_blocks)
         m = lax.rem(i + 2 * lax.rem(lax.div(y + 1, 2), 2), 4)
         swapped = last + lax.div(m, 2) + lax.rem(m, 2) * (3 - 2 * lax.div(m, 2))
-        return i + lax.div(i, last) * (swapped - i)
+        return i + lax.div(i, last) * (swapped - i) + early * (first - i)
 
     def work(i, carry):
+        @pl.when(i == 2)
+        def _():
+            bytes_of(kv.at[:, pl.ds(0, WINDOW), :], r_halo).wait()
+
         pl.when(i == n_blocks - 2)(send_back)
         h = source(turn(i))
         bytes_of(qg.at[h], r_qg.at[h]).wait()

time: 75.8 us -> 75.7 us (level)
  the two profiles are of different devices: /device:TPU:1 before, /device:TPU:31 now
where the time goes in v6:
time: 75.7 us; the launch traced here: 75.6 us
  Pallas kernels  75 us (99%)
    pallas_call x1, Pallas kernels, on_device(): pl.pallas_call(body, out_shape=(pltpu.VMEM(query.shape, BF16), pltpu.VMEM...  73.6 us

profile of v6, /device:TPU:31, one launch (start us, length us, event | category | flops | bytes accessed | tf_op | source)
XLA Modules:
  0.0 75.6 jit_solution(10685231721937494307)
XLA Ops:
  0.6 73.6 %window_attention_grads.1 = (bf16[128,4096]{1,0:T(8,128)(2,1)S(1)}, bf16[128,2048]{1,0:T(8,128)(2,1)S(1)}, bf16[128,2048]{1,0:T(8,128)(2,1)S(1)}) custom-call(bf16[128,4096]{1,0:T(8,128)(2,1)} %refs_0_.1, bf16[128,2048]{1,0:T(8,128)(2,1)} %refs_1_.1, bf16[128,2048]{1,0:T(8,128)(2,1)} %refs_2_.1, bf16[128,4096]{1,0:T(8,128)(2,1)} %refs_3_.1, s32[9,512]{1,0:T(8,128)} %bitcast.1), custom_call_target="tpu_custom_call" | custom-call | tf_op jit(solution)/shard_map/window_attention_grads/pallas_call | solution.py:347
  74.3 1.3 %put_out.1 = (bf16[128,4096]{1,0:T(8,128)(2,1)}, bf16[128,2048]{1,0:T(8,128)(2,1)}, bf16[128,2048]{1,0:T(8,128)(2,1)}) custom-call(bf16[128,4096]{1,0:T(8,128)(2,1)S(1)} %get-tuple-element.6.a, bf16[128,2048]{1,0:T(8,128)(2,1)S(1)} %get-tuple-element.7.b, bf16[128,2048]{1,0:T(8,128)(2,1)S(1)} %get-tuple-element.8.c), custom_call_target="tpu_custom_call" | custom-call | tf_op jit(solution)/shard_map/put_out/pallas_call | solution.py:377
